TPU v7x, 32 devices: a whole 2x2x4 slice. The times are simulated.
32 devices in a mesh: dp: 8 (over z, x), mp: 4 (over y, core).
Axes of the slice: x: 2, y: 2, z: 4, core: 2. Of those that a mesh axis runs over, the one named last changes fastest.
Arguments:
- tokens: bfloat16 [32768, 1024], P('dp'), may hold values from -12 to 12
- out_grad: bfloat16 [32768, 1024], P('dp'), may hold values from -12 to 12
- qk_weight: float32 [2, 1024, 256], P(None, 'dp'), may hold values from -0.1875 to 0.1875
- qk_first: float32 [2, 1024, 256], P(None, 'dp'), may hold values from -0.0048828125 to 0.0048828125
- qk_second: float32 [2, 1024, 256], P(None, 'dp'), may hold values from 5.839972e-07 to 2.3359887e-06
- qk_average: float32 [2, 1024, 256], P(None, 'dp'), may hold values from -0.1875 to 0.1875
- value_weight: float32 [1024, 1024], P('dp', 'mp'), may hold values from -0.1875 to 0.1875
- value_first: float32 [1024, 1024], P('dp', 'mp'), may hold values from -0.0024414062 to 0.0024414062
- value_second: float32 [1024, 1024], P('dp', 'mp'), may hold values from 1.9069296e-07 to 7.6277183e-07
- value_average: float32 [1024, 1024], P('dp', 'mp'), may hold values from -0.1875 to 0.1875
- output_weight: float32 [1024, 1024], P('mp', 'dp'), may hold values from -1.5 to 1.5
- output_first: float32 [1024, 1024], P('mp', 'dp'), may hold values from -0.00048828125 to 0.00048828125
- output_second: float32 [1024, 1024], P('mp', 'dp'), may hold values from 6.7040493e-09 to 2.6816197e-08
- output_average: float32 [1024, 1024], P('mp', 'dp'), may hold values from -1.5 to 1.5
- gate_up_weight: float32 [2, 1024, 2752], P(None, 'dp', 'mp'), may hold values from -0.1875 to 0.1875
- gate_up_first: float32 [2, 1024, 2752], P(None, 'dp', 'mp'), may hold values from -0.0009765625 to 0.0009765625
- gate_up_second: float32 [2, 1024, 2752], P(None, 'dp', 'mp'), may hold values from 3.2775354e-08 to 1.3110142e-07
- gate_up_average: float32 [2, 1024, 2752], P(None, 'dp', 'mp'), may hold values from -0.1875 to 0.1875
- down_weight: float32 [2752, 1024], P('mp', 'dp'), may hold values from -0.109375 to 0.109375
- down_first: float32 [2752, 1024], P('mp', 'dp'), may hold values from -0.001953125 to 0.001953125
- down_second: float32 [2752, 1024], P('mp', 'dp'), may hold values from 1.0726479e-07 to 4.2905916e-07
- down_average: float32 [2752, 1024], P('mp', 'dp'), may hold values from -0.109375 to 0.109375
- gains: float32 [2, 1024], P(None, 'dp'), may hold values from 0.5 to 1.5
- gains_first: float32 [2, 1024], P(None, 'dp'), may hold values from -0.0034179688 to 0.0034179688
- gains_second: float32 [2, 1024], P(None, 'dp'), may hold values from 2.9795777e-07 to 1.1918311e-06
- gains_average: float32 [2, 1024], P(None, 'dp'), may hold values from 0.5 to 1.5
Outputs:
- block_out: bfloat16 [32768, 1024], P('dp', 'mp')
- input_grad: float32 [32768, 1024], P('dp', 'mp')
- grad_norm: float32 [], replicated
- qk_first_new: float32 [2, 1024, 256], P(None, 'dp')
- qk_second_new: float32 [2, 1024, 256], P(None, 'dp')
- qk_new: float32 [2, 1024, 256], P(None, 'dp')
- qk_average_new: float32 [2, 1024, 256], P(None, 'dp')
- value_first_new: float32 [1024, 1024], P('dp', 'mp')
- value_second_new: float32 [1024, 1024], P('dp', 'mp')
- value_new: float32 [1024, 1024], P('dp', 'mp')
- value_average_new: float32 [1024, 1024], P('dp', 'mp')
- output_first_new: float32 [1024, 1024], P('mp', 'dp')
- output_second_new: float32 [1024, 1024], P('mp', 'dp')
- output_new: float32 [1024, 1024], P('mp', 'dp')
- output_average_new: float32 [1024, 1024], P('mp', 'dp')
- gate_up_first_new: float32 [2, 1024, 2752], P(None, 'dp', 'mp')
- gate_up_second_new: float32 [2, 1024, 2752], P(None, 'dp', 'mp')
- gate_up_new: float32 [2, 1024, 2752], P(None, 'dp', 'mp')
- gate_up_average_new: float32 [2, 1024, 2752], P(None, 'dp', 'mp')
- down_first_new: float32 [2752, 1024], P('mp', 'dp')
- down_second_new: float32 [2752, 1024], P('mp', 'dp')
- down_new: float32 [2752, 1024], P('mp', 'dp')
- down_average_new: float32 [2752, 1024], P('mp', 'dp')
- gains_first_new: float32 [2, 1024], P(None, 'dp')
- gains_second_new: float32 [2, 1024], P(None, 'dp')
- gains_new: float32 [2, 1024], P(None, 'dp')
- gains_average_new: float32 [2, 1024], P(None, 'dp')
All inputs are finite; a program needn't handle non-finite values.
Results may differ from a plain program's by a relative error of at most 0.018.
Values may be sent and summed in bfloat16 or wider, within the bound.
A program may use at most 256 MiB of HBM per device.

v0:
```python
import math

import jax
import jax.numpy as jnp
from jax import lax
from jax.sharding import PartitionSpec as P

D = 1024
H = 16
F = 16
VH = 64
FF = 2752
V_ALL = 1024
LEN = 1024
STEP = 5


def inner(left, right):
    return lax.dot_general(
        left, right, (((0,), (0,)), ((), ())), preferred_element_type=jnp.float32
    )


def against(left, right):
    return lax.dot_general(
        left, right, (((1,), (1,)), ((), ())), preferred_element_type=jnp.float32
    )


def rms_scale(values):
    return lax.rsqrt(jnp.mean(values * values, axis=1, keepdims=True) + 1e-05)


def score_table(query, keys):
    length = query.shape[0]
    causal = (jnp.arange(length)[:, None] >= jnp.arange(length)[None, :]).astype(jnp.float32)
    tiled = jnp.einsum("ihf,jhf->hij", query, keys, preferred_element_type=jnp.float32) / math.sqrt(
        query.shape[2]
    )
    return (tiled, causal)


def mix_forward(parts):
    query, keys, values = parts
    tiled, causal = score_table(query, keys)
    kernel = causal * (1.0 + tiled + 0.5 * tiled * tiled)
    numer = jnp.einsum(
        "hij,jhv->ihv", kernel.astype(jnp.bfloat16), values, preferred_element_type=jnp.float32
    )
    return (numer, jnp.sum(kernel, axis=2).T)


def mix_backward(parts):
    query, keys, values, numer, denom, grad_mixed = parts
    tiled, causal = score_table(query, keys)
    kernel = causal * (1.0 + tiled + 0.5 * tiled * tiled)
    grad_numer = (grad_mixed / denom[:, :, None]).astype(jnp.bfloat16)
    grad_denom = -jnp.sum(grad_mixed * numer, axis=2) / (denom * denom)
    grad_kernel = (
        jnp.einsum("ihv,jhv->hij", grad_numer, values, preferred_element_type=jnp.float32)
        + grad_denom.T[:, :, None]
    )
    grad_tiled = (causal * grad_kernel * (1.0 + tiled)).astype(jnp.bfloat16)
    root = math.sqrt(query.shape[2])
    grad_values = jnp.einsum(
        "hij,ihv->jhv", kernel.astype(jnp.bfloat16), grad_numer, preferred_element_type=jnp.float32
    ).astype(jnp.bfloat16)
    grad_query = (
        jnp.einsum("hij,jhf->ihf", grad_tiled, keys, preferred_element_type=jnp.float32) / root
    ).astype(jnp.bfloat16)
    grad_keys = (
        jnp.einsum("hij,ihf->jhf", grad_tiled, query, preferred_element_type=jnp.float32) / root
    ).astype(jnp.bfloat16)
    return (grad_query, grad_keys, grad_values)


def adam_step(grad, first, second, weight, average, rate):
    first = 0.5 * first + 0.5 * grad
    second = 0.5 * second + 0.5 * grad * grad
    correct = 1.0 - 0.5**STEP
    weight = weight - rate * (first / correct / (jnp.sqrt(second / correct) + 1e-08) + 0.1 * weight)
    average = 0.5 * average + 0.5 * weight
    return (first, second, weight, average)


def on_device(
    tokens,
    out_grad,
    qk_weight,
    qk_first,
    qk_second,
    qk_average,
    value_weight,
    value_first,
    value_second,
    value_average,
    output_weight,
    output_first,
    output_second,
    output_average,
    gate_up_weight,
    gate_up_first,
    gate_up_second,
    gate_up_average,
    down_weight,
    down_first,
    down_second,
    down_average,
    gains,
    gains_first,
    gains_second,
    gains_average,
):
    groups = lax.axis_size("mp")
    rank = lax.axis_index("mp")
    qk_full, value_local, output_local, gate_up_local, down_local, gains_full = (
        lax.all_gather(qk_weight.astype(jnp.bfloat16), "dp", axis=1, tiled=True),
        lax.all_gather(value_weight.astype(jnp.bfloat16), "dp", axis=0, tiled=True),
        lax.all_gather(output_weight.astype(jnp.bfloat16), "dp", axis=1, tiled=True),
        lax.all_gather(gate_up_weight.astype(jnp.bfloat16), "dp", axis=1, tiled=True),
        lax.all_gather(down_weight.astype(jnp.bfloat16), "dp", axis=1, tiled=True),
        lax.all_gather(gains.astype(jnp.bfloat16), "dp", axis=1, tiled=True),
    )
    width = qk_full.shape[2] // groups
    qk_local = lax.dynamic_slice_in_dim(qk_full, rank * width, width, 2)
    tok_count = tokens.shape[0]
    seq_count = tok_count // LEN
    heads_here = H // groups
    cols = tokens.shape[1] // groups
    col_start = rank * cols
    first_gain = gains_full[0].astype(jnp.float32)
    second_gain = gains_full[1].astype(jnp.float32)
    inputs = tokens.astype(jnp.float32)
    scale_one = rms_scale(inputs)
    normed_one = inputs * scale_one
    hidden_one = (normed_one * first_gain).astype(jnp.bfloat16)
    query = jnp.dot(hidden_one, qk_local[0], preferred_element_type=jnp.float32).astype(
        jnp.bfloat16
    )
    keys = jnp.dot(hidden_one, qk_local[1], preferred_element_type=jnp.float32).astype(jnp.bfloat16)
    values = jnp.dot(hidden_one, value_local, preferred_element_type=jnp.float32).astype(
        jnp.bfloat16
    )
    head_query = query.reshape(seq_count, LEN, heads_here, F)
    head_keys = keys.reshape(seq_count, LEN, heads_here, F)
    head_values = values.reshape(seq_count, LEN, heads_here, VH)
    numer, denom = lax.map(mix_forward, (head_query, head_keys, head_values))
    mixed = (numer / denom[:, :, :, None]).astype(jnp.bfloat16).reshape(tok_count, heads_here * VH)
    attn_part = jnp.dot(mixed, output_local, preferred_element_type=jnp.float32)
    resid = inputs + lax.psum(attn_part.astype(jnp.bfloat16), "mp").astype(jnp.float32)
    scale_two = rms_scale(resid)
    normed_two = resid * scale_two
    hidden_two = (normed_two * second_gain).astype(jnp.bfloat16)
    gate = jnp.dot(hidden_two, gate_up_local[0], preferred_element_type=jnp.float32)
    lift = jnp.dot(hidden_two, gate_up_local[1], preferred_element_type=jnp.float32)
    sigma = jax.nn.sigmoid(gate)
    activ = (gate * sigma * lift).astype(jnp.bfloat16)
    down_part = jnp.dot(activ, down_local, preferred_element_type=jnp.float32)
    block_out = (
        lax.dynamic_slice_in_dim(resid, col_start, cols, 1)
        + lax.psum_scatter(
            down_part.astype(jnp.bfloat16), "mp", scatter_dimension=1, tiled=True
        ).astype(jnp.float32)
    ).astype(jnp.bfloat16)
    cotan = out_grad.astype(jnp.float32)
    grad_activ = against(out_grad, down_local)
    down_grad = inner(activ, out_grad)
    grad_gate = (grad_activ * lift * sigma * (1.0 + gate * (1.0 - sigma))).astype(jnp.bfloat16)
    grad_lift = (grad_activ * gate * sigma).astype(jnp.bfloat16)
    gate_up_grad = jnp.stack((inner(hidden_two, grad_gate), inner(hidden_two, grad_lift)))
    back_two = lax.psum(
        (against(grad_gate, gate_up_local[0]) + against(grad_lift, gate_up_local[1])).astype(
            jnp.bfloat16
        ),
        "mp",
    ).astype(jnp.float32)
    gain_two = jnp.sum(back_two * normed_two, axis=0)
    grad_resid = (
        cotan
        + scale_two * second_gain * back_two
        - resid * scale_two**3 * jnp.mean(resid * second_gain * back_two, axis=1, keepdims=True)
    )
    resid_low = grad_resid.astype(jnp.bfloat16)
    output_grad = inner(mixed, resid_low)
    grad_mixed = against(resid_low, output_local).reshape(seq_count, LEN, heads_here, VH)
    grad_query, grad_keys, grad_values = lax.map(
        mix_backward, (head_query, head_keys, head_values, numer, denom, grad_mixed)
    )
    grad_query = grad_query.reshape(tok_count, width)
    grad_keys = grad_keys.reshape(tok_count, width)
    grad_values = grad_values.reshape(tok_count, heads_here * VH)
    qk_grad = jnp.stack((inner(hidden_one, grad_query), inner(hidden_one, grad_keys)))
    value_grad = inner(hidden_one, grad_values)
    back_one = (
        against(grad_query, qk_local[0])
        + against(grad_keys, qk_local[1])
        + against(grad_values, value_local)
    )
    input_part = scale_one * first_gain * back_one - inputs * scale_one**3 * jnp.mean(
        inputs * first_gain * back_one, axis=1, keepdims=True
    )
    gains_grad = jnp.stack((jnp.sum(back_one * normed_one, axis=0), gain_two))
    input_grad = lax.dynamic_slice_in_dim(grad_resid, col_start, cols, 1) + lax.psum_scatter(
        input_part.astype(jnp.bfloat16), "mp", scatter_dimension=1, tiled=True
    ).astype(jnp.float32)
    qk_grad = lax.all_gather(qk_grad.astype(jnp.bfloat16), "mp", axis=2, tiled=True).astype(
        qk_grad.dtype
    )
    qk_share, value_share, output_share, gate_up_share, down_share, gains_share = (
        lax.psum_scatter(qk_grad, "dp", scatter_dimension=1, tiled=True),
        lax.psum_scatter(value_grad, "dp", scatter_dimension=0, tiled=True),
        lax.psum_scatter(output_grad, "dp", scatter_dimension=1, tiled=True),
        lax.psum_scatter(gate_up_grad, "dp", scatter_dimension=1, tiled=True),
        lax.psum_scatter(down_grad, "dp", scatter_dimension=1, tiled=True),
        lax.psum_scatter(gains_grad, "dp", scatter_dimension=1, tiled=True),
    )
    first_row = lax.psum(gains_share[0], "mp")
    gains_share = jnp.stack((first_row, gains_share[1]))
    spread_sum = (
        jnp.sum(value_share * value_share)
        + jnp.sum(output_share * output_share)
        + jnp.sum(gate_up_share * gate_up_share)
        + jnp.sum(down_share * down_share)
    )
    shared_sum = jnp.sum(qk_share * qk_share) + jnp.sum(gains_share * gains_share)
    total = lax.psum(spread_sum + shared_sum / groups, ("dp", "mp"))
    grad_norm = jnp.sqrt(total)
    clip = jnp.minimum(1.0, 1.0 / (grad_norm + 1e-06))
    qk_m, qk_v, qk_w, qk_a = adam_step(
        clip * qk_share, qk_first, qk_second, qk_weight, qk_average, 1.0 / math.sqrt(D)
    )
    value_m, value_v, value_w, value_a = adam_step(
        clip * value_share,
        value_first,
        value_second,
        value_weight,
        value_average,
        1.0 / math.sqrt(D),
    )
    output_m, output_v, output_w, output_a = adam_step(
        clip * output_share,
        output_first,
        output_second,
        output_weight,
        output_average,
        1.0 / math.sqrt(max(1, V_ALL * 16 // LEN)),
    )
    gate_up_m, gate_up_v, gate_up_w, gate_up_a = adam_step(
        clip * gate_up_share,
        gate_up_first,
        gate_up_second,
        gate_up_weight,
        gate_up_average,
        1.0 / math.sqrt(D),
    )
    down_m, down_v, down_w, down_a = adam_step(
        clip * down_share, down_first, down_second, down_weight, down_average, 1.0 / math.sqrt(FF)
    )
    gains_m, gains_v, gains_w, gains_a = adam_step(
        clip * gains_share, gains_first, gains_second, gains, gains_average, 0.4
    )
    return (
        block_out,
        input_grad,
        grad_norm,
        qk_m,
        qk_v,
        qk_w,
        qk_a,
        value_m,
        value_v,
        value_w,
        value_a,
        output_m,
        output_v,
        output_w,
        output_a,
        gate_up_m,
        gate_up_v,
        gate_up_w,
        gate_up_a,
        down_m,
        down_v,
        down_w,
        down_a,
        gains_m,
        gains_v,
        gains_w,
        gains_a,
    )


def solution(mesh):
    placed = (
        P("dp", None),
        P("dp", None),
        P(None, "dp", None),
        P(None, "dp", None),
        P(None, "dp", None),
        P(None, "dp", None),
        P("dp", "mp"),
        P("dp", "mp"),
        P("dp", "mp"),
        P("dp", "mp"),
        P("mp", "dp"),
        P("mp", "dp"),
        P("mp", "dp"),
        P("mp", "dp"),
        P(None, "dp", "mp"),
        P(None, "dp", "mp"),
        P(None, "dp", "mp"),
        P(None, "dp", "mp"),
        P("mp", "dp"),
        P("mp", "dp"),
        P("mp", "dp"),
        P("mp", "dp"),
        P(None, "dp"),
        P(None, "dp"),
        P(None, "dp"),
        P(None, "dp"),
    )
    return jax.shard_map(
        on_device,
        mesh=mesh,
        in_specs=placed,
        out_specs=(
            P("dp", "mp"),
            P("dp", "mp"),
            P(),
            P(None, "dp", None),
            P(None, "dp", None),
            P(None, "dp", None),
            P(None, "dp", None),
            P("dp", "mp"),
            P("dp", "mp"),
            P("dp", "mp"),
            P("dp", "mp"),
            P("mp", "dp"),
            P("mp", "dp"),
            P("mp", "dp"),
            P("mp", "dp"),
            P(None, "dp", "mp"),
            P(None, "dp", "mp"),
            P(None, "dp", "mp"),
            P(None, "dp", "mp"),
            P("mp", "dp"),
            P("mp", "dp"),
            P("mp", "dp"),
            P("mp", "dp"),
            P(None, "dp"),
            P(None, "dp"),
            P(None, "dp"),
            P(None, "dp"),
        ),
        check_vma=False,
    )
```

profile of v0, /device:TPU:0, one launch (start us, length us, event | category | flops | bytes accessed | tf_op | source)
XLA Modules:
  0.0 1489.0 jit_solution(11503148982517520819)
XLA Ops:
  9.9 22.2 %all_gather.21 = bf16[2,1024]{1,0:T(2,128)(2,1)S(1)} all-gather(bf16[2,128]{1,0:T(2,128)(2,1)S(1)} %convert_element_type.163), channel_id=1, replica_groups=mesh['dp'=8,'mp'=4] {'dp'}, dimensions={1}, use_global_device_ids=true | all-gather | bytes 4608 | tf_op jit(solution)/shard_map/all_gather | solution.py:122
  32.2 5.1 fusion.56
  37.9 31.9 %all_gather.22 = bf16[1024,256]{1,0:T(8,128)(2,1)S(1)} all-gather(bf16[128,256]{1,0:T(8,128)(2,1)S(1)} %convert_element_type.165), channel_id=1, replica_groups=mesh['dp'=8,'mp'=4] {'dp'}, dimensions={0}, use_global_device_ids=true | all-gather | bytes 589824 | tf_op jit(solution)/shard_map/all_gather | solution.py:118
  80.9 5.6 copy.95
  86.5 28.1 %all_gather.24 = bf16[256,1024]{1,0:T(8,128)(2,1)} all-gather(bf16[256,128]{1,0:T(8,128)(2,1)S(1)} %convert_element_type.171), channel_id=1, replica_groups=mesh['dp'=8,'mp'=4] {'dp'}, dimensions={1}, use_global_device_ids=true | all-gather | bytes 589824 | tf_op jit(solution)/shard_map/all_gather | solution.py:119
  114.6 6.1 convolution_convert_fusion.3
  121.3 6.1 convolution_convert_fusion.4
  129.8 35.0 %while.30 = (s32[]{:T(128)}, f32[4,1024,4,64]{1,3,2,0:T(8,128)}, f32[4,1024,4]{1,2,0:T(4,128)S(1)}, bf16[4,1024,4,64]{1,3,2,0:T(8,128)(2,1)S(1)}, bf16[4,1024,4,...) while((s32[]{:T(128)}, f32[4,1024,4,64]{1,3,2,0:T(8,128)}, ...), condition=%wide.region_3.4_spmd, body=%wide.region_1.3_spmd.sunk | while | flops 706736128 | bytes 27052120 | solution.py:147
  130.5 5.6 fusion.150
  139.2 5.6 fusion.150
  147.9 5.6 fusion.150
  156.6 5.6 fusion.150
  164.8 4.0 divide_convert_fusion.3
  172.6 5.7 convolution_convert_fusion.1
  181.0 148.5 %all-reduce.3.cloned.1.call-done = bf16[4096,1024]{1,0:T(8,128)(2,1)} async-done(((bf16[4096,1024]{1,0:T(8,128)(2,1)}), bf16[4096,1024]{1,0:T(8,128)(2,1)}) %all-reduce.3.cloned.1.call-update) | async-done | bytes 8388624 | tf_op jit(solution)/shard_map/psum | solution.py:150
  329.6 8.6 multiply_reduce_fusion
  338.1 10.8 multiply_convert_fusion.9
  348.9 42.7 %all-gather.7.cloned.1.call-done = bf16[2,1024,688]{1,2,0:T(8,128)(2,1)} async-done(((bf16[2,128,688]{1,2,0:T(8,128)(2,1)}), bf16[2,1024,688]{1,2,0:T(8,128)(2,1)}) %all-gather.7.cloned.1.call-update) | async-done | bytes 2818064 | tf_op jit(solution)/shard_map/all_gather | solution.py:120
  391.6 12.5 fusion.68
  404.1 8.8 fusion.67
  412.9 22.6 %all-gather.9.cloned.1.call-done = bf16[688,1024]{1,0:T(8,128)(2,1)} async-done(((bf16[688,128]{1,0:T(8,128)(2,1)}), bf16[688,1024]{1,0:T(8,128)(2,1)}) %all-gather.9.cloned.1.call-update) | async-done | bytes 1409040 | tf_op jit(solution)/shard_map/all_gather | solution.py:121
  435.5 22.1 %multiply_convert_fusion.10 = (bf16[4096,688]{0,1:T(8,128)(2,1)}, bf16[4096,688]{0,1:T(8,128)(2,1)}, bf16[4096,688]{0,1:T(8,128)(2,1)}) fusion(f32[4096,688]{0,1:T(8,128)} %fusion.67, f32[4096,688]{0,1:T(8,128)} %fusion.68, bf16[4096,1024]{1,0:T(8,128)(2,1)} %param.31, bf16[688,1024]{1,0:T(8,128)(2,1)} %all-gather.9.cloned.1.call-done), kind=kOutput, calls=%fused_computation.84 | convolution fusion | flops 5816451072 | bytes 49250304 | tf_op jit(solution)/shard_map/dot_general | solution.py:25
  457.6 13.2 fusion.66
  470.8 12.5 add_convert_fusion
  483.4 151.4 %all-reduce.5.cloned.1.call-done = bf16[4096,1024]{1,0:T(8,128)(2,1)} async-done(((bf16[4096,1024]{1,0:T(8,128)(2,1)}), bf16[4096,1024]{1,0:T(8,128)(2,1)}) %all-reduce.5.cloned.1.call-update) | async-done | bytes 8388624 | tf_op jit(solution)/shard_map/psum | solution.py:171
  634.8 12.0 fusion.55
  646.8 17.5 %fusion.53 = (f32[4096,1024]{1,0:T(8,128)S(1)}, f32[4096,1024]{1,0:T(8,128)}) fusion(bf16[4096,1024]{1,0:T(8,128)(2,1)} %all-reduce.5.cloned.1.call-done, bf16[4096,1024]{1,0:T(8,128)(2,1)} %param.31, f32[4096]{0:T(1024)S(1)} %broadcast_multiply_fusion.1, f32[4096]{0:T(1024)S(1)} %get-tuple-element.439, f32[1024]{0:T(1024)S(1)} %bitcast.225, ...), kind=kLoop, calls=%fused_computation.71 | loop fusion | flops 46137344 | bytes 67162112 | tf_op jit(solution)/shard_map/sub | solution.py:179
  664.3 5.7 copy-done.5
  670.1 4.4 fusion.64
  674.4 6.0 reshape.148
  680.5 141.2 %while.31 = (s32[]{:T(128)}, bf16[4,1024,4,16]{1,3,2,0:T(8,128)(2,1)}, bf16[4,1024,4,16]{1,3,2,0:T(8,128)(2,1)}, bf16[4,1024,4,64]{1,3,2,0:T(8,128)(2,1)}, bf16[...) while((s32[]{:T(128)}, ...), condition=%wide.region_11.12_spmd, body=%wide.region_9.11_spmd.sunk | while | flops 1535123456 | bytes 167644336 | solution.py:186
  690.7 5.7 copy-done
  696.4 4.8 fusion.165
  701.1 8.3 multiply_convert_fusion.16
  725.8 5.7 copy-done
  731.5 4.7 fusion.165
  736.3 8.3 multiply_convert_fusion.16
  761.0 5.7 copy-done
  766.7 4.7 fusion.165
  771.4 8.3 multiply_convert_fusion.16
  796.2 5.7 copy-done
  801.9 4.7 fusion.165
  806.6 8.3 multiply_convert_fusion.16
  832.6 9.6 fusion.75
  842.3 9.3 fusion.74
  851.6 18.5 %fusion.51 = (f32[1024]{0:T(1024)S(1)}, f32[4096]{0:T(1024)S(1)}, f32[4096,1024]{1,0:T(8,128)}) fusion(bf16[4096,1024]{1,0:T(8,128)(2,1)S(1)} %bitcast.205, f32[4096]{0:T(1024)S(1)} %copy-done.29, f32[1024]{0:T(1024)S(1)} %bitcast.221, bf16[4096,256]{0,1:T(8,128)(2,1)S(1)} %bitcast.208, bf16[1024,256]{1,0:T(8,128)(2,1)} %copy-done.19, ...), kind=kOutput, calls=%fused_computation.69 | convolution fusion | flops 2185227264 | bytes 61382656 | tf_op jit(solution)/shard_map/dot_general | solution.py:25
  871.2 11.6 fusion.92
  882.9 9.2 fusion.62
  892.1 7.4 fusion.91
  902.5 10.3 convolution_bitcast_fusion
  912.8 10.1 convolution_bitcast_fusion.1
  926.0 11.8 convolution_convert_fusion
  938.5 12.5 fusion.59
  953.7 6.1 psum.30
  960.4 50.7 %reduce-scatter.21.cloned.1.call-done = f32[688,128]{1,0:T(8,128)} async-done(((f32[688,1024]{1,0:T(8,128)}), f32[688,128]{1,0:T(8,128)}) %reduce-scatter.21.cloned.1.call-update) | async-done | bytes 352272 | tf_op jit(solution)/shard_map/reduce_scatter | solution.py:214
  1012.9 64.5 %reduce-scatter.17.cloned.1.call-done = f32[256,128]{1,0:T(8,128)} async-done(((f32[256,1024]{1,0:T(8,128)}), f32[256,128]{1,0:T(8,128)}) %reduce-scatter.17.cloned.1.call-update) | async-done | bytes 131088 | tf_op jit(solution)/shard_map/reduce_scatter | solution.py:212
  1078.9 64.1 %reduce-scatter.15.cloned.1.call-done = f32[128,256]{1,0:T(8,128)} async-done(((f32[1024,256]{1,0:T(8,128)}), f32[128,256]{1,0:T(8,128)}) %reduce-scatter.15.cloned.1.call-update) | async-done | bytes 131088 | tf_op jit(solution)/shard_map/reduce_scatter | solution.py:211
  1145.9 69.1 %reduce-scatter.23.cloned.1.call-done = f32[2,128,256]{1,2,0:T(8,128)} async-done(((f32[2,1024,256]{1,2,0:T(8,128)}), f32[2,128,256]{1,2,0:T(8,128)}) %reduce-scatter.23.cloned.1.call-update) | async-done | bytes 262160 | tf_op jit(solution)/shard_map/reduce_scatter | solution.py:210
  1217.9 108.5 %reduce-scatter.19.cloned.1.call-done = f32[2,128,688]{1,2,0:T(8,128)} async-done(((f32[2,1024,688]{1,2,0:T(8,128)}), f32[2,128,688]{1,2,0:T(8,128)}) %reduce-scatter.19.cloned.1.call-update) | async-done | bytes 704528 | tf_op jit(solution)/shard_map/reduce_scatter | solution.py:213
  1329.7 40.8 %psum.31 = f32[]{:T(128)} all-reduce(f32[]{:T(128)S(6)} %add.280), channel_id=1, replica_groups=mesh['dp'=8,'mp'=4] {'dp','mp'}, use_global_device_ids=true, to_apply=%region_29.30 | all-reduce | flops 1 | bytes 8 | tf_op jit(solution)/shard_map/psum | solution.py:226
  1390.8 10.6 reduce-scatter.11.cloned.1.call-done
  1401.4 4.6 add_convert_fusion.1
  1406.0 69.6 %reduce-scatter.13.cloned.1.call-done = bf16[4096,256]{1,0:T(8,128)(2,1)} async-done(((bf16[4096,1024]{1,0:T(8,128)(2,1)}), bf16[4096,256]{1,0:T(8,128)(2,1)}) %reduce-scatter.13.cloned.1.call-update) | async-done | bytes 2097168 | tf_op jit(solution)/shard_map/reduce_scatter | solution.py:203
  1475.6 5.2 convert_add_fusion.1
  (230 shorter events, 151.4 us)
Async XLA Ops:
  7.2 30.7 %copy-start.24 = (f32[128,256]{1,0:T(8,128)S(1)}, f32[128,256]{1,0:T(8,128)}, u32[]{:S(2)}) copy-start(f32[128,256]{1,0:T(8,128)} %param.36) | copy-start | bytes 393220
  7.2 30.7 %copy-start.26 = (f32[256,128]{1,0:T(8,128)S(1)}, f32[256,128]{1,0:T(8,128)}, u32[]{:S(2)}) copy-start(f32[256,128]{1,0:T(8,128)} %param.40) | copy-start | bytes 393220
  7.2 107.4 %all-gather.5.cloned.1.call-start = ((), (), s32[]{:S(2)}) async-start(), calls=%async_computation.8 | async-start | bytes 1179648 | tf_op jit(solution)/shard_map/all_gather | solution.py:117
  9.0 320.6 %all-reduce.3.cloned.1.call-start = ((), (), s32[]{:S(2)}) async-start(), calls=%async_computation.9 | async-start | bytes 16777216 | tf_op jit(solution)/shard_map/psum | solution.py:150
  9.0 60.8 %copy-start.1 = (bf16[4096,1024]{1,0:T(8,128)(2,1)S(1)}, bf16[4096,1024]{1,0:T(8,128)(2,1)}, u32[]{:S(2)}) copy-start(bf16[4096,1024]{1,0:T(8,128)(2,1)} %param.30) | copy-start | bytes 25165828
  32.2 40.0 %copy-start.34 = (f32[1,1024]{1,0:T(1,128)}, f32[1,1024]{1,0:T(1,128)S(1)}, u32[]{:S(2)}) copy-start(f32[1,1024]{1,0:T(1,128)S(1)} %get-tuple-element.441) | copy-start | bytes 12292
  37.9 32.0 %copy-start.28 = (f32[4096]{0:T(1024)}, f32[4096]{0:T(1024)S(1)}, u32[]{:S(2)}) copy-start(f32[4096]{0:T(1024)S(1)} %get-tuple-element.438) | copy-start | bytes 49156
  69.9 2.3 copy-start.19
  72.1 3.2 copy-start.2
  164.8 6.5 copy-start.30
  164.8 13.5 copy-start.6
  164.8 13.5 copy-start.12
  164.8 13.5 copy-start.13
  164.8 7.8 copy-start.14
  171.3 1.3 copy-start.7
  178.3 2.0 copy-start.20
  178.3 1.2 copy-start.16
  178.3 213.3 %all-gather.7.cloned.1.call-start = ((), (), s32[]{:S(2)}) async-start(), calls=%async_computation.10 | async-start | bytes 3170304 | tf_op jit(solution)/shard_map/all_gather | solution.py:120
  180.2 255.3 %all-gather.9.cloned.1.call-start = ((), (), s32[]{:S(2)}) async-start(), calls=%async_computation.11 | async-start | bytes 1585152 | tf_op jit(solution)/shard_map/all_gather | solution.py:121
  181.0 453.8 %all-reduce.5.cloned.1.call-start = ((), (), s32[]{:S(2)}) async-start(), calls=%async_computation.13 | async-start | bytes 16777216 | tf_op jit(solution)/shard_map/psum | solution.py:171
  391.6 12.5 copy-start.10
  391.6 12.5 copy-start.40
  457.6 13.2 copy-start.42
  483.3 416.3 %all-gather.11.cloned.1.call-start = ((), (), s32[]{:S(2)}) async-start(), calls=%async_computation.19 | async-start | bytes 1310720 | tf_op jit(solution)/shard_map/all_gather | solution.py:206
  646.8 23.2 %copy-start.15 = (bf16[256,1024]{1,0:T(8,128)(2,1)S(1)}, bf16[256,1024]{1,0:T(8,128)(2,1)}, u32[]{:S(2)}) copy-start(bf16[256,1024]{1,0:T(8,128)(2,1)} %all_gather.24) | copy-start | bytes 1572868
  664.3 5.7 copy-start.5
  684.1 6.5 copy-start.4
  690.6 5.7 copy-start
  719.3 6.5 copy-start.4
  725.8 5.7 copy-start
  754.5 6.5 copy-start.4
  761.0 5.7 copy-start
  789.6 6.5 copy-start.4
  796.2 5.7 copy-start
  821.7 6.3 copy-start.3
  825.9 25.6 %copy-start.9 = (bf16[32,8,4,1024]{3,1,2,0:T(8,128)(2,1)}, bf16[32,8,4,1024]{3,1,2,0:T(8,128)(2,1)S(1)}, u32[]{:S(2)}) copy-start(bf16[32,8,4,1024]{3,1,2,0:T(8,128)(2,1)S(1)} %copy.128) | copy-start | bytes 6291460
  828.0 1.6 copy-start.27
  830.2 1.6 copy-start.11
  832.6 120.0 %reduce-scatter.25.cloned.1.call-start = ((), (), s32[]{:S(2)}) async-start(), calls=%async_computation.21 | async-start | bytes 589824
  832.6 18.9 %slice-start = ((s8[8388608]{0:T(1024)(128)(4,1)}), s8[4194304]{0:T(1024)(128)(4,1)S(1)}, s32[]{:S(2)}) async-start(s8[8388608]{0:T(1024)(128)(4,1)} %bitcast.204), calls=%async_computation.22 | async-start | bytes 8388608
  842.3 9.3 slice-start.1
  842.3 9.3 copy-start.29
  842.3 9.3 copy-start.35
  851.6 18.5 %copy-start.37 = (f32[1024]{0:T(1024)S(1)}, f32[1024]{0:T(1024)}, u32[]{:S(2)}) copy-start(f32[1024]{0:T(1024)} %get-tuple-element.368) | copy-start | bytes 12292
  871.1 140.0 %reduce-scatter.21.cloned.1.call-start = ((), (), s32[]{:S(2)}) async-start(), calls=%async_computation.18 | async-start | bytes 3170304 | tf_op jit(solution)/shard_map/reduce_scatter | solution.py:214
  871.2 11.7 copy-start.8
  882.9 194.5 %reduce-scatter.17.cloned.1.call-start = ((), (), s32[]{:S(2)}) async-start(), calls=%async_computation.16 | async-start | bytes 1179648 | tf_op jit(solution)/shard_map/reduce_scatter | solution.py:212
  892.1 250.9 %reduce-scatter.15.cloned.1.call-start = ((), (), s32[]{:S(2)}) async-start(), calls=%async_computation.15 | async-start | bytes 1179648 | tf_op jit(solution)/shard_map/reduce_scatter | solution.py:211
  899.6 315.4 %reduce-scatter.23.cloned.1.call-start = ((), (), s32[]{:S(2)}) async-start(), calls=%async_computation.20 | async-start | bytes 2359296 | tf_op jit(solution)/shard_map/reduce_scatter | solution.py:210
  902.5 423.9 %reduce-scatter.19.cloned.1.call-start = ((), (), s32[]{:S(2)}) async-start(), calls=%async_computation.17 | async-start | bytes 6340608 | tf_op jit(solution)/shard_map/reduce_scatter | solution.py:213
  922.9 3.1 copy-start.41
  926.0 475.4 %reduce-scatter.11.cloned.1.call-start = ((), (), s32[]{:S(2)}) async-start(), calls=%async_computation.12 | async-start | bytes 10485760 | tf_op jit(solution)/shard_map/reduce_scatter | solution.py:161
  937.8 537.8 %reduce-scatter.13.cloned.1.call-start = ((), (), s32[]{:S(2)}) async-start(), calls=%async_computation.14 | async-start | bytes 10485760 | tf_op jit(solution)/shard_map/reduce_scatter | solution.py:203
  951.0 0.9 copy-start.23
  951.0 1.1 copy-start.31
  951.0 1.2 copy-start.32
  951.0 1.4 copy-start.33
  951.0 429.8 %copy-start.25 = (f32[128,256]{1,0:T(8,128)S(1)}, f32[128,256]{1,0:T(8,128)}, u32[]{:S(2)}) copy-start(f32[128,256]{1,0:T(8,128)} %param.36) | copy-start | bytes 393220
  951.1 433.7 %copy-start.21 = (f32[688,128]{1,0:T(8,128)S(1)}, f32[688,128]{1,0:T(8,128)}, u32[]{:S(2)}) copy-start(f32[688,128]{1,0:T(8,128)} %param.48) | copy-start | bytes 1056772
  951.1 436.2 %copy-start.17 = (f32[2,128,688]{1,2,0:T(8,128)S(1)}, f32[2,128,688]{1,2,0:T(8,128)}, u32[]{:S(2)}) copy-start(f32[2,128,688]{1,2,0:T(8,128)} %param.44) | copy-start | bytes 2113540
  953.7 417.5 %copy-start.38 = (f32[1,128]{1,0:T(1,128)}, f32[1,128]{1,0:T(1,128)S(1)}, u32[]{:S(2)}) copy-start(f32[1,128]{1,0:T(1,128)S(1)} %copy.124) | copy-start | bytes 1540
  959.8 411.4 %copy-start.39 = (f32[1,128]{1,0:T(1,128)}, f32[1,128]{1,0:T(1,128)S(1)}, u32[]{:S(2)}) copy-start(f32[1,128]{1,0:T(1,128)S(1)} %psum.30) | copy-start | bytes 1540
  1011.1 373.6 %copy-start.22 = (f32[688,128]{1,0:T(8,128)S(1)}, f32[688,128]{1,0:T(8,128)}, u32[]{:S(2)}) copy-start(f32[688,128]{1,0:T(8,128)} %reduce-scatter.21.cloned.1.call-done) | copy-start | bytes 1056772
  1326.4 60.9 %copy-start.18 = (f32[2,128,688]{1,2,0:T(8,128)S(1)}, f32[2,128,688]{1,2,0:T(8,128)}, u32[]{:S(2)}) copy-start(f32[2,128,688]{1,2,0:T(8,128)} %reduce-scatter.19.cloned.1.call-done) | copy-start | bytes 2113540
  (1 other events, 0.7 us)
Sparse Core Ops, SparseCore 0:
  10.8 46.0 all-gather.4
  178.4 151.0 all-reduce.2
  332.2 59.3 all-gather.6
  394.1 41.3 all-gather.8
  483.5 151.3 all-reduce.4
  832.7 16.8 all-gather.10
  871.3 62.0 reduce-scatter.24
  937.9 73.2 reduce-scatter.20
  1014.9 62.3 reduce-scatter.16
  1080.6 62.3 reduce-scatter.14
  1147.6 67.3 reduce-scatter.22
  1218.9 107.4 reduce-scatter.18
  1329.2 72.2 reduce-scatter.10
  1403.8 71.7 reduce-scatter.12
where the time goes:
time: 1500 us; the launch traced here: 1490 us
  waiting for transfers between devices  802 us (53%)
  matrix products  319 us (21%)
  other arithmetic  131 us (9%)
  blocking collectives  129 us (9%)
  local copies, waits for them, and re-layouts  84.8 us (6%)
  between operations  20.9 us (1%)
    psum x1, waiting for transfers between devices, on_device(): lax.psum((against(grad_gate, gate_up_local[0]) + against(grad_lift, gate_...  151 us
    psum x1, waiting for transfers between devices, on_device(): lax.psum(attn_part.astype(jnp.bfloat16), 'mp').astype(jnp.float32)  149 us
    reduce_scatter x1, waiting for transfers between devices, on_device(): lax.psum_scatter(gate_up_grad, 'dp', scatter_dimension=1, tiled=True)  108 us
    dot_general x7, matrix products, against(): lax.dot_general(left, right, (((1,), (1,)), ((), ())), preferred_element_...  89.6 us
    reduce_scatter x1, waiting for transfers between devices, on_device(): lax.psum_scatter(input_part.astype(jnp.bfloat16), 'mp', scatter_dimension...  69.6 us
    reduce_scatter x1, waiting for transfers between devices, on_device(): lax.psum_scatter(qk_grad, 'dp', scatter_dimension=1, tiled=True)  69.1 us
    reduce_scatter x1, waiting for transfers between devices, on_device(): lax.psum_scatter(output_grad, 'dp', scatter_dimension=1, tiled=True)  64.5 us
    reduce_scatter x1, waiting for transfers between devices, on_device(): lax.psum_scatter(value_grad, 'dp', scatter_dimension=0, tiled=True)  64.1 us
  transfers between devices with their start and end apart: 14, of which 11 were waited for; matrix products, arithmetic and copies ran while one was open for 14% of the time, Pallas kernels for 0%

commit v1 on v0

v1 whole, which is shorter than its diff:
```python
import functools
import math

import jax
import jax.numpy as jnp
from jax import lax
from jax.experimental import pallas as pl
from jax.experimental.pallas import tpu as pltpu
from jax.sharding import PartitionSpec as P

D = 1024
H = 16
F = 16
VH = 64
FF = 2752
V_ALL = 1024
LEN = 1024
STEP = 5
BLOCK = 256


def nn(left, right):
    return lax.dot_general(
        left, right, (((1,), (0,)), ((), ())), preferred_element_type=jnp.float32
    )


def nt(left, right):
    return lax.dot_general(
        left, right, (((1,), (1,)), ((), ())), preferred_element_type=jnp.float32
    )


def tn(left, right):
    return lax.dot_general(
        left, right, (((0,), (0,)), ((), ())), preferred_element_type=jnp.float32
    )


def rms_scale(values):
    return lax.rsqrt(jnp.mean(values * values, axis=1, keepdims=True) + 1e-05)


def upper(size):
    rows = lax.broadcasted_iota(jnp.int32, (size, size), 0)
    return rows <= lax.broadcasted_iota(jnp.int32, (size, size), 1)


def spans(block):
    start = block * BLOCK
    whole = [(0, start, False)] if block else []
    return whole + [(start, start + BLOCK, True)]


def mix_forward(query_ref, keys_ref, values_ref, mixed_ref, denom_ref):
    keys = keys_ref[...].T
    seen = upper(BLOCK)
    for block in range(query_ref.shape[1] // BLOCK):
        at = slice(block * BLOCK, (block + 1) * BLOCK)
        query = query_ref[:, at] * jnp.bfloat16(1.0 / math.sqrt(F))
        numer, denom = 0.0, 0.0
        for low, high, edge in spans(block):
            slope = nn(keys[low:high], query) + 1.0
            kernel = slope * slope + 1.0
            if edge:
                kernel = jnp.where(seen, kernel, 0.0)
            denom += jnp.sum(kernel, axis=0, keepdims=True)
            numer += nn(values_ref[:, low:high], kernel.astype(jnp.bfloat16))
        mixed_ref[:, at] = (numer / denom).astype(jnp.bfloat16)
        denom_ref[0, :, at] = denom


def mix_backward(
    query_ref,
    keys_ref,
    values_ref,
    mixed_ref,
    denom_ref,
    grad_ref,
    grad_query_ref,
    grad_keys_ref,
    grad_values_ref,
    keys_sum,
    values_sum,
):
    root = 1.0 / math.sqrt(F)
    keys = keys_ref[...].T
    values = values_ref[...].T
    seen = upper(BLOCK)
    keys_sum[...] = jnp.zeros_like(keys_sum)
    values_sum[...] = jnp.zeros_like(values_sum)
    for block in range(query_ref.shape[1] // BLOCK):
        at = slice(block * BLOCK, (block + 1) * BLOCK)
        query = query_ref[:, at] * jnp.bfloat16(root)
        share = 2.0 / denom_ref[0, :, at]
        grad = grad_ref[:, at].astype(jnp.float32)
        grad_numer = (grad * share).astype(jnp.bfloat16)
        grad_denom = -share * jnp.sum(
            grad * mixed_ref[:, at].astype(jnp.float32), axis=0, keepdims=True
        )
        grad_query = 0.0
        for low, high, edge in spans(block):
            slope = nn(keys[low:high], query) + 1.0
            kernel = slope * slope + 1.0
            grad_tiled = (nn(values[low:high], grad_numer) + grad_denom) * slope
            if edge:
                kernel = jnp.where(seen, kernel, 0.0)
                grad_tiled = jnp.where(seen, grad_tiled, 0.0)
            kernel = kernel.astype(jnp.bfloat16)
            grad_tiled = grad_tiled.astype(jnp.bfloat16)
            values_sum[:, low:high] += nt(grad_numer, kernel)
            keys_sum[:, low:high] += nt(query, grad_tiled)
            grad_query += nn(keys_ref[:, low:high], grad_tiled)
        grad_query_ref[:, at] = (grad_query * root).astype(jnp.bfloat16)
    grad_keys_ref[...] = keys_sum[...].astype(jnp.bfloat16)
    grad_values_ref[...] = (values_sum[...] * 0.5).astype(jnp.bfloat16)


def head_specs(groups, count):
    here = H // groups
    small = here * (2 * F + VH) // F
    large = here * (2 * F + VH) // VH
    skip = 2 * here * F // VH
    query = pl.BlockSpec((F, count), lambda h: (h // here * small + h % here, 0))
    keys = pl.BlockSpec((F, count), lambda h: (h // here * small + here + h % here, 0))
    values = pl.BlockSpec((VH, count), lambda h: (h // here * large + skip + h % here, 0))
    return [query, keys, values]


def attend(projected, groups):
    count = projected.shape[1]
    return pl.pallas_call(
        mix_forward,
        grid=(H,),
        in_specs=head_specs(groups, count),
        out_specs=[
            pl.BlockSpec((VH, count), lambda h: (h, 0)),
            pl.BlockSpec((1, 1, count), lambda h: (h, 0, 0)),
        ],
        out_shape=[
            jax.ShapeDtypeStruct((H * VH, count), jnp.bfloat16),
            jax.ShapeDtypeStruct((H, 1, count), jnp.float32),
        ],
        cost_estimate=pl.CostEstimate(
            flops=20_000_000_000, bytes_accessed=8_000_000, transcendentals=0
        ),
        compiler_params=pltpu.CompilerParams(vmem_limit_bytes=48 << 20),
        name="attend",
    )(projected, projected, projected)


def attend_back(projected, mixed, denom, grad, groups):
    count = projected.shape[1]
    head = pl.BlockSpec((VH, count), lambda h: (h, 0))
    return pl.pallas_call(
        mix_backward,
        grid=(H,),
        in_specs=head_specs(groups, count)
        + [head, pl.BlockSpec((1, 1, count), lambda h: (h, 0, 0)), head],
        out_specs=[
            pl.BlockSpec((F, count), lambda h: (h, 0)),
            pl.BlockSpec((F, count), lambda h: (h, 0)),
            head,
        ],
        out_shape=[
            jax.ShapeDtypeStruct((H * F, count), jnp.bfloat16),
            jax.ShapeDtypeStruct((H * F, count), jnp.bfloat16),
            jax.ShapeDtypeStruct((H * VH, count), jnp.bfloat16),
        ],
        scratch_shapes=[
            pltpu.VMEM((F, count), jnp.float32),
            pltpu.VMEM((VH, count), jnp.float32),
        ],
        cost_estimate=pl.CostEstimate(
            flops=40_000_000_000, bytes_accessed=12_000_000, transcendentals=0
        ),
        compiler_params=pltpu.CompilerParams(vmem_limit_bytes=48 << 20),
        name="attend_back",
    )(projected, projected, projected, mixed, denom, grad)


def adam_step(grad, first, second, weight, average, rate):
    first = 0.5 * first + 0.5 * grad
    second = 0.5 * second + 0.5 * grad * grad
    correct = 1.0 - 0.5**STEP
    weight = weight - rate * (first / correct / (jnp.sqrt(second / correct) + 1e-08) + 0.1 * weight)
    average = 0.5 * average + 0.5 * weight
    return (first, second, weight, average)


def gather(shard):
    return lax.all_gather(
        lax.all_gather(shard, "dp", axis=1, tiled=True), "mp", axis=0, tiled=True
    )


def scatter(grad):
    return lax.psum_scatter(
        lax.psum_scatter(grad, "mp", scatter_dimension=0, tiled=True),
        "dp",
        scatter_dimension=1,
        tiled=True,
    )


def on_device(
    tokens,
    out_grad,
    qk_weight,
    qk_first,
    qk_second,
    qk_average,
    value_weight,
    value_first,
    value_second,
    value_average,
    output_weight,
    output_first,
    output_second,
    output_average,
    gate_up_weight,
    gate_up_first,
    gate_up_second,
    gate_up_average,
    down_weight,
    down_first,
    down_second,
    down_average,
    gains,
    gains_first,
    gains_second,
    gains_average,
):
    groups = lax.axis_size("mp")
    rank = lax.axis_index("mp")
    low = jnp.bfloat16
    here = H // groups
    count = tokens.shape[0] // groups
    assert count == LEN
    width = here * F
    qk_here = lax.dynamic_slice_in_dim(qk_weight, rank * width, width, 2).astype(low)
    shard_in = jnp.concatenate((qk_here[0].T, qk_here[1].T, value_weight.astype(low).T), axis=0)
    w_in = gather(shard_in)
    w_out = gather(output_weight.astype(low))
    w_gate = gather(gate_up_weight[0].astype(low).T)
    w_up = gather(gate_up_weight[1].astype(low).T)
    w_down = gather(down_weight.astype(low))
    gains_full = lax.all_gather(gains.astype(low), "dp", axis=1, tiled=True).astype(jnp.float32)
    first_gain, second_gain = gains_full[0], gains_full[1]

    inputs = lax.dynamic_slice_in_dim(tokens, rank * count, count, 0).astype(jnp.float32)
    cotan_low = lax.dynamic_slice_in_dim(out_grad, rank * count, count, 0)
    cotan = cotan_low.astype(jnp.float32)
    scale_one = rms_scale(inputs)
    hidden_one = (inputs * scale_one * first_gain).astype(low)
    projected = nt(w_in, hidden_one).astype(low)
    mixed, denom = attend(projected, groups)
    resid = inputs + tn(mixed, w_out)
    scale_two = rms_scale(resid)
    hidden_two = (resid * scale_two * second_gain).astype(low)
    gate = nt(w_gate, hidden_two)
    lift = nt(w_up, hidden_two)
    sigma = jax.nn.sigmoid(gate)
    grad_activ = nt(w_down, cotan_low)
    activ = (gate * sigma * lift).astype(low)
    grad_gate = (grad_activ * lift * sigma * (1.0 + gate * (1.0 - sigma))).astype(low)
    grad_lift = (grad_activ * gate * sigma).astype(low)
    down_grad = nn(activ, cotan_low).astype(low)
    gate_grad = nn(grad_gate, hidden_two).astype(low)
    up_grad = nn(grad_lift, hidden_two).astype(low)
    block_out = (resid + tn(activ, w_down)).astype(low)
    back_two = tn(grad_gate, w_gate) + tn(grad_lift, w_up)
    gain_two = jnp.sum(back_two * resid * scale_two, axis=0)
    grad_resid = (
        cotan
        + scale_two * second_gain * back_two
        - resid * scale_two**3 * jnp.mean(resid * second_gain * back_two, axis=1, keepdims=True)
    )
    resid_low = grad_resid.astype(low)
    output_grad = nn(mixed, resid_low).astype(low)
    grad_mixed = nt(w_out, resid_low).astype(low)
    grad_query, grad_keys, grad_values = attend_back(projected, mixed, denom, grad_mixed, groups)
    pieces = []
    for group in range(groups):
        pieces += [
            grad_query[group * width : (group + 1) * width],
            grad_keys[group * width : (group + 1) * width],
            grad_values[group * here * VH : (group + 1) * here * VH],
        ]
    grad_projected = jnp.concatenate(pieces, axis=0)
    in_grad = nn(grad_projected, hidden_one).astype(low)
    back_one = tn(grad_projected, w_in)
    gain_one = jnp.sum(back_one * inputs * scale_one, axis=0)
    input_grad = (
        grad_resid
        + scale_one * first_gain * back_one
        - inputs * scale_one**3 * jnp.mean(inputs * first_gain * back_one, axis=1, keepdims=True)
    ).astype(low)

    block_out = lax.all_to_all(block_out, "mp", split_axis=1, concat_axis=0, tiled=True)
    input_grad = lax.all_to_all(input_grad, "mp", split_axis=1, concat_axis=0, tiled=True).astype(
        jnp.float32
    )
    down_share = scatter(down_grad).astype(jnp.float32)
    gate_share = scatter(gate_grad).astype(jnp.float32)
    up_share = scatter(up_grad).astype(jnp.float32)
    output_share = scatter(output_grad).astype(jnp.float32)
    in_share = scatter(in_grad).astype(jnp.float32)
    gains_grad = lax.psum(jnp.stack((gain_one, gain_two)), "mp")
    gains_share = lax.psum_scatter(gains_grad, "dp", scatter_dimension=1, tiled=True)

    total = lax.psum(
        jnp.sum(down_share * down_share)
        + jnp.sum(gate_share * gate_share)
        + jnp.sum(up_share * up_share)
        + jnp.sum(output_share * output_share)
        + jnp.sum(in_share * in_share)
        + jnp.sum(gains_share * gains_share) / groups,
        ("dp", "mp"),
    )
    grad_norm = jnp.sqrt(total)
    clip = jnp.minimum(1.0, 1.0 / (grad_norm + 1e-06))
    qk_part = jnp.stack((in_share[:width].T, in_share[width : 2 * width].T)).astype(low)
    qk_share = lax.all_gather(qk_part, "mp", axis=2, tiled=True).astype(jnp.float32)
    value_share = in_share[2 * width :].T
    gate_up_share = jnp.stack((gate_share.T, up_share.T))
    root = 1.0 / math.sqrt(D)
    outs = ()
    for share, first, second, weight, average, rate in (
        (qk_share, qk_first, qk_second, qk_weight, qk_average, root),
        (value_share, value_first, value_second, value_weight, value_average, root),
        (
            output_share,
            output_first,
            output_second,
            output_weight,
            output_average,
            1.0 / math.sqrt(max(1, V_ALL * 16 // LEN)),
        ),
        (gate_up_share, gate_up_first, gate_up_second, gate_up_weight, gate_up_average, root),
        (down_share, down_first, down_second, down_weight, down_average, 1.0 / math.sqrt(FF)),
        (gains_share, gains_first, gains_second, gains, gains_average, 0.4),
    ):
        outs += adam_step(clip * share, first, second, weight, average, rate)
    return (block_out, input_grad, grad_norm) + outs


def solution(mesh):
    placed = (
        P("dp", None),
        P("dp", None),
        P(None, "dp", None),
        P(None, "dp", None),
        P(None, "dp", None),
        P(None, "dp", None),
        P("dp", "mp"),
        P("dp", "mp"),
        P("dp", "mp"),
        P("dp", "mp"),
        P("mp", "dp"),
        P("mp", "dp"),
        P("mp", "dp"),
        P("mp", "dp"),
        P(None, "dp", "mp"),
        P(None, "dp", "mp"),
        P(None, "dp", "mp"),
        P(None, "dp", "mp"),
        P("mp", "dp"),
        P("mp", "dp"),
        P("mp", "dp"),
        P("mp", "dp"),
        P(None, "dp"),
        P(None, "dp"),
        P(None, "dp"),
        P(None, "dp"),
    )
    return jax.shard_map(
        on_device,
        mesh=mesh,
        in_specs=placed,
        out_specs=(
            P("dp", "mp"),
            P("dp", "mp"),
            P(),
            P(None, "dp", None),
            P(None, "dp", None),
            P(None, "dp", None),
            P(None, "dp", None),
            P("dp", "mp"),
            P("dp", "mp"),
            P("dp", "mp"),
            P("dp", "mp"),
            P("mp", "dp"),
            P("mp", "dp"),
            P("mp", "dp"),
            P("mp", "dp"),
            P(None, "dp", "mp"),
            P(None, "dp", "mp"),
            P(None, "dp", "mp"),
            P(None, "dp", "mp"),
            P("mp", "dp"),
            P("mp", "dp"),
            P("mp", "dp"),
            P("mp", "dp"),
            P(None, "dp"),
            P(None, "dp"),
            P(None, "dp"),
            P(None, "dp"),
        ),
        check_vma=False,
    )
```

time: 1500 us -> 1140 us (0.76)
  matrix products: 319 us -> 144 us
  waiting for transfers between devices: 802 us -> 670 us
  other arithmetic: 131 us -> 29.4 us
  Pallas kernels: 0 us -> 57.2 us
  local copies, waits for them, and re-layouts: 84.8 us -> 68.6 us
    unnamed x15 -> x25, waiting for transfers between devices: 0.25 us -> 344 us
    psum x2 -> x0, waiting for transfers between devices: 300 us -> none  [the longest x1 151 us: on_device(): lax.psum((against(grad_gate, gate_up_local[0]) + against(grad_lift, gate_...]
    reduce_scatter x7 -> x5, waiting for transfers between devices: 437 us -> 159 us  [scatter(): lax.psum_scatter(grad, 'mp', scatter_dimension=0, tiled=True)]
    dot_general x49 -> x15, matrix products: 319 us -> 144 us  [the longest x5 56.7 us: nt(): lax.dot_general(left, right, (((1,), (1,)), ((), ())), preferred_element_...]
    all_gather x4 -> x8, waiting for transfers between devices: 65.2 us -> 167 us  [the longest x5 125 us: gather(): lax.all_gather(lax.all_gather(shard, 'dp', axis=1, tiled=True), 'mp', axi...]
    pallas_call x0 -> x2, Pallas kernels: none -> 57.2 us  [the longest x1 37.2 us: attend_back(): pl.pallas_call(mix_backward, grid=(H,), in_specs=head_specs(groups, count...]
    while x22 -> x0, local copies, waits for them, and re-layouts: 35.4 us -> none
    convert_element_type x20 -> x7, other arithmetic: 45 us -> 11.8 us  [the longest x1 5.95 us: on_device(): input_grad = (grad_resid + scale_one * first_gain * back_one - inputs * s...]
  transfers between devices with their start and end apart: 14 -> 21, of which waited for: 11 -> 15; matrix products, arithmetic and copies ran while one was open for 14% -> 14% of each run, Pallas kernels for 0% -> 5%
where the time goes in v1:
time: 1140 us
  waiting for transfers between devices  670 us (59%)
  matrix products  144 us (13%)
  blocking collectives  136 us (12%)
  local copies, waits for them, and re-layouts  68.6 us (6%)
  Pallas kernels  57.2 us (5%)
  other arithmetic  29.4 us (3%)
  between operations  20.6 us (2%)
    unnamed x25, waiting for transfers between devices  344 us
    reduce_scatter x5, waiting for transfers between devices, scatter(): lax.psum_scatter(grad, 'mp', scatter_dimension=0, tiled=True)  159 us
    all_gather x5, waiting for transfers between devices, gather(): lax.all_gather(lax.all_gather(shard, 'dp', axis=1, tiled=True), 'mp', axi...  125 us
    all_gather x2, blocking collectives, gather(): lax.all_gather(shard, 'dp', axis=1, tiled=True)  66.9 us
    dot_general x5, matrix products, nt(): lax.dot_general(left, right, (((1,), (1,)), ((), ())), preferred_element_...  56.7 us
    unnamed x108, local copies, waits for them, and re-layouts  54.4 us
    dot_general x5, matrix products, tn(): lax.dot_general(left, right, (((0,), (0,)), ((), ())), preferred_element_...  46.1 us
    all_gather x3, waiting for transfers between devices, gather(): lax.all_gather(shard, 'dp', axis=1, tiled=True)  42 us
  transfers between devices with their start and end apart: 21, of which 15 were waited for; matrix products, arithmetic and copies ran while one was open for 14% of the time, Pallas kernels for 5%

profile of v1, /device:TPU:0, one launch (start us, length us, event | category | flops | bytes accessed | tf_op | source)
XLA Modules:
  0.0 1135.8 jit_solution(12736342004880298820)
XLA Ops:
  10.0 1.7 convert_element_type.119
  13.8 36.6 %all_gather.36 = bf16[384,1024]{0,1:T(8,128)(2,1)} all-gather(bf16[384,128]{0,1:T(8,128)(2,1)S(1)} %pad_maximum_fusion), channel_id=1, replica_groups=mesh['dp'=8,'mp'=4] {'dp'}, dimensions={1}, use_global_device_ids=true | all-gather | bytes 884736 | tf_op jit(solution)/shard_map/all_gather | solution.py:193
  50.5 30.3 %all_gather.39 = bf16[256,1024]{1,0:T(8,128)(2,1)} all-gather(bf16[256,128]{1,0:T(8,128)(2,1)S(1)} %convert_element_type.114), channel_id=1, replica_groups=mesh['dp'=8,'mp'=4] {'dp'}, dimensions={1}, use_global_device_ids=true | all-gather | bytes 589824 | tf_op jit(solution)/shard_map/all_gather | solution.py:193
  81.5 29.9 %all-gather.13.cloned.1.call-done = bf16[688,1024]{1,0:T(8,128)(2,1)} async-done(((bf16[688,128]{1,0:T(8,128)(2,1)}), bf16[688,1024]{1,0:T(8,128)(2,1)}) %all-gather.13.cloned.1.call-update) | async-done | bytes 1409040 | tf_op jit(solution)/shard_map/all_gather | solution.py:193
  111.5 3.1 constant_dynamic-slice_fusion.1
  114.6 2.9 copy.112
  117.5 3.9 constant_dynamic-slice_fusion
  121.3 3.9 copy.113
  125.3 18.0 %all_gather.38 = bf16[2,1024]{1,0:T(2,128)(2,1)S(1)} all-gather(bf16[2,128]{1,0:T(2,128)(2,1)S(1)} %convert_element_type.110), channel_id=1, replica_groups=mesh['dp'=8,'mp'=4] {'dp'}, dimensions={1}, use_global_device_ids=true | all-gather | bytes 4608 | tf_op jit(solution)/shard_map/all_gather | solution.py:248
  143.8 12.0 %all-gather.21.cloned.1.call-done = bf16[688,1024]{1,0:T(8,128)(2,1)} async-done(((bf16[688,128]{1,0:T(8,128)(2,1)}), bf16[688,1024]{1,0:T(8,128)(2,1)}) %all-gather.21.cloned.1.call-update) | async-done | bytes 1409040 | tf_op jit(solution)/shard_map/all_gather | solution.py:193
  157.1 27.2 %all-gather.9.cloned.1.call-done = bf16[1536,1024]{0,1:T(8,128)(2,1)} async-done(((bf16[384,1024]{0,1:T(8,128)(2,1)}), bf16[1536,1024]{0,1:T(8,128)(2,1)}) %all-gather.9.cloned.1.call-update) | async-done | bytes 3145744 | tf_op jit(solution)/shard_map/all_gather | solution.py:192
  184.3 5.7 convolution_convert_fusion.4.query_ref.keys_ref.values_ref
  190.0 20.0 %attend.1 = (bf16[1024,1024]{1,0:T(8,128)(2,1)S(1)}, f32[16,1,1024]{2,1,0:T(1,128)S(1)}) custom-call(bf16[1536,1024]{1,0:T(8,128)(2,1)S(1)} %convolution_convert_fusion.4.query_ref.keys_ref.values_ref, bf16[1536,1024]{1,0:T(8,128)(2,1)S(1)} %convolution_convert_fusion.4.query_ref.keys_ref.values_ref, ...), custom_call_target="tpu_custom_call" | custom-call | flops 20000000000 | bytes 8000000 | tf_op jit(solution)/shard_map/attend/pallas_call | solution.py:132
  211.6 4.8 multiply_reduce_fusion.2
  216.4 2.0 copy-done.3
  218.4 1.7 multiply_convert_fusion
  220.1 32.3 %all-gather.19.cloned.1.call-done = bf16[2752,1024]{1,0:T(8,128)(2,1)} async-done(((bf16[688,1024]{1,0:T(8,128)(2,1)}), bf16[2752,1024]{1,0:T(8,128)(2,1)}) %all-gather.19.cloned.1.call-update) | async-done | bytes 5636112 | tf_op jit(solution)/shard_map/all_gather | solution.py:192
  252.4 11.6 %fusion.44 = f32[1024,2752]{0,1:T(8,128)} fusion(bf16[2752,1024]{1,0:T(8,128)(2,1)} %all-gather.19.cloned.1.call-done, bf16[1024,1024]{0,1:T(8,128)(2,1)} %multiply_convert_fusion), kind=kOutput, calls=%fused_computation.131 | convolution fusion | flops 5771362304 | bytes 19005440 | tf_op jit(solution)/shard_map/dot_general | solution.py:29
  264.0 32.7 %all-gather.15.cloned.1.call-done = bf16[2752,1024]{1,0:T(8,128)(2,1)} async-done(((bf16[688,1024]{1,0:T(8,128)(2,1)}), bf16[2752,1024]{1,0:T(8,128)(2,1)}) %all-gather.15.cloned.1.call-update) | async-done | bytes 5636112 | tf_op jit(solution)/shard_map/all_gather | solution.py:192
  296.7 11.6 %fusion.43 = f32[1024,2752]{0,1:T(8,128)} fusion(bf16[2752,1024]{1,0:T(8,128)(2,1)} %all-gather.15.cloned.1.call-done, bf16[1024,1024]{0,1:T(8,128)(2,1)} %multiply_convert_fusion), kind=kOutput, calls=%fused_computation.130 | convolution fusion | flops 5771362304 | bytes 19005440 | tf_op jit(solution)/shard_map/dot_general | solution.py:29
  308.2 32.7 %all-gather.23.cloned.1.call-done = bf16[2752,1024]{1,0:T(8,128)(2,1)} async-done(((bf16[688,1024]{1,0:T(8,128)(2,1)}), bf16[2752,1024]{1,0:T(8,128)(2,1)}) %all-gather.23.cloned.1.call-update) | async-done | bytes 5636112 | tf_op jit(solution)/shard_map/all_gather | solution.py:192
  340.9 21.4 %fusion.4 = (bf16[2752,1024]{1,0:T(8,128)(2,1)}, bf16[2752,1024]{1,0:T(8,128)(2,1)}, bf16[2752,1024]{1,0:T(8,128)(2,1)}) fusion(f32[1024,2752]{0,1:T(8,128)} %fusion.43, f32[1024,2752]{0,1:T(8,128)} %fusion.44, bf16[2752,1024]{1,0:T(8,128)(2,1)} %all-gather.23.cloned.1.call-done, bf16[1024,1024]{1,0:T(8,128)(2,1)} %constant_dynamic-slice_fusion), kind=kOutput, calls=%fused_computation.6 | convolution fusion | flops 5816451072 | bytes 47185920 | tf_op jit(solution)/shard_map/dot_general | solution.py:29
  362.3 11.3 fusion.42
  373.6 9.8 multiply_reduce_fusion
  384.5 2.0 copy-done.5
  386.5 3.7 convolution_convert_fusion.5
  390.3 6.5 convert_bitcast_fusion.1.grad_ref
  396.7 37.2 %attend_back.1 = (bf16[256,1024]{1,0:T(8,128)(2,1)S(1)}, bf16[256,1024]{1,0:T(8,128)(2,1)S(1)}, bf16[1024,1024]{1,0:T(8,128)(2,1)S(1)}) custom-call(bf16[1536,1024]{1,0:T(8,128)(2,1)} %copy-done, bf16[1536,1024]{1,0:T(8,128)(2,1)} %copy-done, bf16[1536,1024]{1,0:T(8,128)(2,1)} %copy-done, bf16[1024,1024]{1,0:T(8,128)(2,1)S(1)} %get-tuple-element.32.mixed_ref, ...), custom_call_target="tpu_custom_call" | custom-call | flops 40000000000 | bytes 12000000 | tf_op jit(solution)/shard_map/attend_back/pallas_call | solution.py:155
  436.3 5.3 convolution_convert_fusion.3
  441.7 10.9 convolution_convert_fusion.1
  452.6 10.6 convolution_convert_fusion.2
  463.3 10.9 convolution_convert_fusion
  474.2 8.7 fusion.19
  484.1 2.0 copy.106
  486.2 2.3 copy.108
  488.7 47.7 %reduce-scatter.26.cloned.1.call-done = bf16[688,1024]{1,0:T(8,128)(2,1)} async-done(((bf16[2752,1024]{1,0:T(8,128)(2,1)}), bf16[688,1024]{1,0:T(8,128)(2,1)}) %reduce-scatter.26.cloned.1.call-update) | async-done | bytes 1409040 | tf_op jit(solution)/shard_map/reduce_scatter | solution.py:199
  536.4 2.6 copy.102
  539.0 54.0 %reduce-scatter.24.cloned.1.call-done = bf16[688,1024]{1,0:T(8,128)(2,1)} async-done(((bf16[2752,1024]{1,0:T(8,128)(2,1)}), bf16[688,1024]{1,0:T(8,128)(2,1)}) %reduce-scatter.24.cloned.1.call-update) | async-done | bytes 1409040 | tf_op jit(solution)/shard_map/reduce_scatter | solution.py:199
  593.0 2.6 copy.100
  595.6 5.9 fusion.15
  601.6 3.7 all-to-all-start.1
  605.3 57.4 %reduce-scatter.28.cloned.1.call-done = bf16[688,1024]{1,0:T(8,128)(2,1)} async-done(((bf16[2752,1024]{1,0:T(8,128)(2,1)}), bf16[688,1024]{1,0:T(8,128)(2,1)}) %reduce-scatter.28.cloned.1.call-update) | async-done | bytes 1409040 | tf_op jit(solution)/shard_map/reduce_scatter | solution.py:199
  662.8 2.7 copy.104
  665.5 11.5 %add_convert_fusion = bf16[1024,1024]{0,1:T(8,128)(2,1)} fusion(f32[1024,1024]{0,1:T(8,128)} %copy-done.3, bf16[2752,1024]{1,0:T(8,128)(2,1)} %get-tuple-element.121, bf16[2752,1024]{1,0:T(8,128)(2,1)} %all-gather.23.cloned.1.call-done), kind=kOutput, calls=%fused_computation.39 | convolution fusion | flops 5773459456 | bytes 17563648 | tf_op jit(solution)/shard_map/dot_general | solution.py:35
  677.0 4.6 all-to-all-start
  687.0 41.7 %reduce-scatter.44.cloned.1.call-done = f32[128,2]{1,0:T(8,128)} async-done(((f32[1024,2]{1,0:T(8,128)}), f32[128,2]{1,0:T(8,128)}) %reduce-scatter.44.cloned.1.call-update) | async-done | bytes 1040
  729.6 5.7 psum.16
  736.5 2.5 convert_bitcast_fusion
  739.0 5.4 copy.80
  744.4 4.0 copy.77
  748.4 45.2 %reduce-scatter.40.cloned.1.call-done = bf16[128,256]{1,0:T(8,128)(2,1)} async-done(((bf16[1024,256]{1,0:T(8,128)(2,1)}), bf16[128,256]{1,0:T(8,128)(2,1)}) %reduce-scatter.40.cloned.1.call-update) | async-done | bytes 65552
  795.1 63.4 %reduce-scatter.42.cloned.1.call-done = bf16[128,384]{1,0:T(8,128)(2,1)} async-done(((bf16[1024,384]{1,0:T(8,128)(2,1)}), bf16[128,384]{1,0:T(8,128)(2,1)}) %reduce-scatter.42.cloned.1.call-update) | async-done | bytes 98320
  859.6 5.4 all_gather.47
  865.7 60.1 %reduce-scatter.36.cloned.1.call-done = bf16[128,688]{1,0:T(8,128)(2,1)} async-done(((bf16[1024,688]{1,0:T(8,128)(2,1)}), bf16[128,688]{1,0:T(8,128)(2,1)}) %reduce-scatter.36.cloned.1.call-update) | async-done | bytes 176144
  926.9 66.3 %reduce-scatter.34.cloned.1.call-done = bf16[128,688]{1,0:T(8,128)(2,1)} async-done(((bf16[1024,688]{1,0:T(8,128)(2,1)}), bf16[128,688]{1,0:T(8,128)(2,1)}) %reduce-scatter.34.cloned.1.call-update) | async-done | bytes 176144
  994.3 66.2 %reduce-scatter.38.cloned.1.call-done = bf16[128,688]{1,0:T(8,128)(2,1)} async-done(((bf16[1024,688]{1,0:T(8,128)(2,1)}), bf16[128,688]{1,0:T(8,128)(2,1)}) %reduce-scatter.38.cloned.1.call-update) | async-done | bytes 176144
  1066.4 39.8 %psum.15 = f32[]{:T(128)} all-reduce(f32[]{:T(128)S(6)} %add.223), channel_id=1, replica_groups=mesh['dp'=8,'mp'=4] {'dp','mp'}, use_global_device_ids=true, to_apply=%region_24.0 | all-reduce | flops 1 | bytes 8 | tf_op jit(solution)/shard_map/psum | solution.py:312
  1106.9 1.8 add_multiply_fusion.4
  1114.5 1.9 copy.91
  1116.4 1.8 copy.92
  1118.2 1.8 copy.93
  1121.4 2.5 add_multiply_fusion.1
  1123.9 1.9 add_multiply_fusion.3
  1125.9 2.0 add_multiply_fusion
  (167 shorter events, 36.0 us)
Async XLA Ops:
  7.2 43.3 %copy-start.15 = (f32[256,128]{1,0:T(8,128)S(1)}, f32[256,128]{1,0:T(8,128)}, u32[]{:S(2)}) copy-start(f32[256,128]{1,0:T(8,128)} %param.36) | copy-start | bytes 393220
  7.2 73.7 %all-gather.17.cloned.1.call-start = ((), (), s32[]{:S(2)}) async-start(), calls=%async_computation.17 | async-start | bytes 1585152 | tf_op jit(solution)/shard_map/all_gather | solution.py:193
  9.2 102.2 %all-gather.13.cloned.1.call-start = ((), (), s32[]{:S(2)}) async-start(), calls=%async_computation.15 | async-start | bytes 1585152 | tf_op jit(solution)/shard_map/all_gather | solution.py:193
  10.0 145.9 %all-gather.21.cloned.1.call-start = ((), (), s32[]{:S(2)}) async-start(), calls=%async_computation.19 | async-start | bytes 1585152 | tf_op jit(solution)/shard_map/all_gather | solution.py:193
  11.7 172.5 %all-gather.9.cloned.1.call-start = ((), (), s32[]{:S(2)}) async-start(), calls=%async_computation.13 | async-start | bytes 3932160 | tf_op jit(solution)/shard_map/all_gather | solution.py:192
  50.5 161.1 %all-gather.11.cloned.1.call-start = ((), (), s32[]{:S(2)}) async-start(), calls=%async_computation.14 | async-start | bytes 2621440 | tf_op jit(solution)/shard_map/all_gather | solution.py:192
  80.8 171.6 %all-gather.19.cloned.1.call-start = ((), (), s32[]{:S(2)}) async-start(), calls=%async_computation.18 | async-start | bytes 7045120 | tf_op jit(solution)/shard_map/all_gather | solution.py:192
  81.4 215.3 %all-gather.15.cloned.1.call-start = ((), (), s32[]{:S(2)}) async-start(), calls=%async_computation.16 | async-start | bytes 7045120 | tf_op jit(solution)/shard_map/all_gather | solution.py:192
  111.4 229.5 %all-gather.23.cloned.1.call-start = ((), (), s32[]{:S(2)}) async-start(), calls=%async_computation.20 | async-start | bytes 7045120 | tf_op jit(solution)/shard_map/all_gather | solution.py:192
  111.5 6.0 copy-start.27
  117.4 66.8 %copy-start.1 = (bf16[1024,1024]{0,1:T(8,128)(2,1)}, bf16[1024,1024]{0,1:T(8,128)(2,1)S(1)}, u32[]{:S(2)}) copy-start(bf16[1024,1024]{0,1:T(8,128)(2,1)S(1)} %copy.112) | copy-start | bytes 6291460
  155.9 328.2 %reduce-scatter.30.cloned.1.call-start = ((), (), s32[]{:S(2)}) async-start(), calls=%async_computation.24 | async-start | bytes 2621440 | tf_op jit(solution)/shard_map/reduce_scatter | solution.py:199
  157.0 27.2 %copy-start.22 = (f32[1024]{0:T(1024)}, f32[1024]{0:T(1024)S(1)}, u32[]{:S(2)}) copy-start(f32[1024]{0:T(1024)S(1)} %get-tuple-element.129) | copy-start | bytes 12292
  157.0 27.2 %copy-start.24 = (f32[1,1024]{1,0:T(1,128)}, f32[1,1024]{1,0:T(1,128)S(1)}, u32[]{:S(2)}) copy-start(f32[1,1024]{1,0:T(1,128)S(1)} %get-tuple-element.133) | copy-start | bytes 12292
  209.9 1.6 copy-start
  216.4 2.0 copy-start.3
  362.3 11.3 copy-start.4
  362.3 11.3 copy-start.32
  373.6 9.9 copy-start.6
  384.5 2.0 copy-start.5
  390.2 96.0 %reduce-scatter.32.cloned.1.call-start = ((), (), s32[]{:S(2)}) async-start(), calls=%async_computation.25 | async-start | bytes 3932160 | tf_op jit(solution)/shard_map/reduce_scatter | solution.py:199
  434.0 2.3 copy-start.2
  434.0 2.3 copy-start.23
  434.0 2.3 copy-start.25
  434.3 1.6 copy-start.26
  441.6 94.8 %reduce-scatter.26.cloned.1.call-start = ((), (), s32[]{:S(2)}) async-start(), calls=%async_computation.22 | async-start | bytes 7045120 | tf_op jit(solution)/shard_map/reduce_scatter | solution.py:199
  452.6 140.4 %reduce-scatter.24.cloned.1.call-start = ((), (), s32[]{:S(2)}) async-start(), calls=%async_computation.21 | async-start | bytes 7045120 | tf_op jit(solution)/shard_map/reduce_scatter | solution.py:199
  463.2 199.5 %reduce-scatter.28.cloned.1.call-start = ((), (), s32[]{:S(2)}) async-start(), calls=%async_computation.23 | async-start | bytes 7045120 | tf_op jit(solution)/shard_map/reduce_scatter | solution.py:199
  474.2 254.6 %reduce-scatter.44.cloned.1.call-start = ((), (), s32[]{:S(2)}) async-start(), calls=%async_computation.31 | async-start | bytes 589824
  484.0 309.5 %reduce-scatter.40.cloned.1.call-start = ((), (), s32[]{:S(2)}) async-start(), calls=%async_computation.29 | async-start | bytes 589824
  486.2 372.4 %reduce-scatter.42.cloned.1.call-start = ((), (), s32[]{:S(2)}) async-start(), calls=%async_computation.30 | async-start | bytes 884736
  488.6 107.0 %copy-start.21 = (f32[1024]{0:T(1024)S(1)}, f32[1024]{0:T(1024)}, u32[]{:S(2)}) copy-start(f32[1024]{0:T(1024)} %get-tuple-element.128) | copy-start | bytes 12292
  488.6 437.2 %reduce-scatter.36.cloned.1.call-start = ((), (), s32[]{:S(2)}) async-start(), calls=%async_computation.27 | async-start | bytes 1769472
  539.0 454.2 %reduce-scatter.34.cloned.1.call-start = ((), (), s32[]{:S(2)}) async-start(), calls=%async_computation.26 | async-start | bytes 1769472
  601.6 75.4 %all-to-all-start.1 = ((bf16[1024,4,256]{0,2,1:T(8,128)(2,1)}), bf16[1024,4,256]{0,2,1:T(8,128)(2,1)S(1)}, u32[]{:S(2)}, u32[]{:S(2)}) async-start(bf16[1024,4,256]{0,2,1:T(8,128)(2,1)} %bitcast.134), calls=%async_computation.1 | async-start | bytes 4194304 | tf_op jit(solution)/shard_map/all_to_all | solution.py:301
  605.3 455.2 %reduce-scatter.38.cloned.1.call-start = ((), (), s32[]{:S(2)}) async-start(), calls=%async_computation.28 | async-start | bytes 1769472
  676.9 4.7 copy-start.14
  676.9 5.4 copy-start.16
  676.9 5.6 copy-start.20
  677.0 9.6 copy-start.17
  677.0 9.8 copy-start.18
  677.0 9.9 copy-start.19
  677.0 67.4 %all-to-all-start = ((bf16[1024,4,256]{0,2,1:T(8,128)(2,1)}), bf16[1024,4,256]{0,2,1:T(8,128)(2,1)}, u32[]{:S(2)}, u32[]{:S(2)}) async-start(bf16[1024,4,256]{0,2,1:T(8,128)(2,1)} %bitcast.141), calls=%async_computation | async-start | bytes 4194304 | tf_op jit(solution)/shard_map/all_to_all | solution.py:300
  744.4 362.5 %copy-start.12 = (f32[128,256]{0,1:T(8,128)S(1)}, f32[128,256]{0,1:T(8,128)}, u32[]{:S(2)}) copy-start(f32[128,256]{0,1:T(8,128)} %copy.89) | copy-start | bytes 393220
  744.4 362.5 %copy-start.13 = (f32[128,256]{0,1:T(8,128)S(1)}, f32[128,256]{0,1:T(8,128)}, u32[]{:S(2)}) copy-start(f32[128,256]{0,1:T(8,128)} %copy.86) | copy-start | bytes 393220
  1060.5 60.3 %copy-start.28 = (f32[2,128]{1,0:T(2,128)S(1)}, f32[2,128]{1,0:T(2,128)}, u32[]{:S(2)}) copy-start(f32[2,128]{1,0:T(2,128)} %param.48) | copy-start | bytes 3076
  1060.5 60.3 %copy-start.29 = (f32[2,128]{1,0:T(2,128)S(1)}, f32[2,128]{1,0:T(2,128)}, u32[]{:S(2)}) copy-start(f32[2,128]{1,0:T(2,128)} %param.51) | copy-start | bytes 3076
  1060.5 60.3 %copy-start.30 = (f32[2,128]{1,0:T(2,128)S(1)}, f32[2,128]{1,0:T(2,128)}, u32[]{:S(2)}) copy-start(f32[2,128]{1,0:T(2,128)} %param.50) | copy-start | bytes 3076
  1060.5 60.3 %copy-start.31 = (f32[2,128]{1,0:T(2,128)S(1)}, f32[2,128]{1,0:T(2,128)}, u32[]{:S(2)}) copy-start(f32[2,128]{1,0:T(2,128)} %param.49) | copy-start | bytes 3076
  1060.5 60.9 %copy-start.8 = (f32[688,128]{1,0:T(8,128)S(1)}, f32[688,128]{1,0:T(8,128)}, u32[]{:S(2)}) copy-start(f32[688,128]{1,0:T(8,128)} %param.44) | copy-start | bytes 1056772
  1113.5 12.4 %copy-start.7 = (f32[2,128,688]{1,2,0:T(8,128)S(1)}, f32[2,128,688]{1,2,0:T(8,128)}, u32[]{:S(2)}) copy-start(f32[2,128,688]{1,2,0:T(8,128)} %param.40) | copy-start | bytes 2113540
  1114.5 11.4 %copy-start.9 = (f32[2,128,688]{1,2,0:T(8,128)S(1)}, f32[2,128,688]{1,2,0:T(8,128)}, u32[]{:S(2)}) copy-start(f32[2,128,688]{1,2,0:T(8,128)} %param.43) | copy-start | bytes 2113540
  1120.8 5.1 copy-start.10
  1120.8 5.1 copy-start.11
Sparse Core Ops, SparseCore 0:
  10.7 50.8 all-gather.16
  64.2 47.1 all-gather.12
  114.0 41.7 all-gather.20
  157.2 26.9 all-gather.8
  185.7 22.5 all-gather.10
  209.7 42.6 all-gather.18
  254.0 42.6 all-gather.14
  298.2 42.6 all-gather.22
  390.3 31.4 reduce-scatter.29
  441.7 37.9 reduce-scatter.31
  482.3 54.0 reduce-scatter.25
  539.0 53.9 reduce-scatter.23
  595.5 67.1 reduce-scatter.27
  666.9 61.8 reduce-scatter.43
  732.5 60.9 reduce-scatter.39
  797.1 61.4 reduce-scatter.41
  861.8 63.9 reduce-scatter.35
  929.4 63.7 reduce-scatter.33
  996.6 63.8 reduce-scatter.37
